TPU v7x, 256 devices: a whole 4x4x8 slice. The times are simulated.
256 devices in a mesh: chan: 8 (over x_lo, y), lon: 32 (over x_hi, z, core).
Axes of the slice: x: 4 (x_hi: 2, x_lo: 2; x = x_hi * 2 + x_lo), y: 4, z: 8, core: 2. Of those that a mesh axis runs over, the one named last changes fastest.
Arguments:
- symbols: int32 [320, 4, 128, 128], P('chan', None, 'lon'), may hold values from -3 to 3
- hyper_mean: bfloat16 [320, 4, 128, 128], P('chan', None, 'lon'), may hold values from -6 to 6
- slice_order: int32 [8], replicated, may hold values from 0 to 7, each once
- hyper_weight: bfloat16 [8, 15, 224, 40], P('chan'), may hold values from -0.25 to 0.25
- ctx_weight: bfloat16 [8, 15, 224, 320], P('chan'), may hold values from -0.09375 to 0.09375
- ctx_bias: float32 [8, 224], P('chan'), may hold values from -6 to 6
- out_weight: bfloat16 [8, 40, 224], P('chan'), may hold values from -0.375 to 0.375
- gdn_beta: float32 [320], replicated, may hold values from 0.5 to 4
- gdn_gamma: float32 [320, 320], replicated, may hold values from 0 to 0.006
- tconv_weight: bfloat16 [27, 64, 320], P(None, 'chan'), may hold values from -0.078125 to 0.078125
Outputs:
- upsampled: bfloat16 [64, 8, 256, 256], P('chan', None, 'lon')
Inputs may be any that keep to these rules, and one draw needn't show every extreme that they name: `slice_order`: each slice number appears exactly once.
All inputs are finite; a program needn't handle non-finite values.
Results may differ from a plain program's by a relative error of at most 0.014.
Values may be sent and summed in bfloat16 or wider, within the bound.
No kernel may reach another device: no remote copies, remote signals or barrier semaphores. Data moves between devices by JAX's collectives and lax.ppermute only.
A program may use at most 64 MiB of HBM per device.

v0:
```python
import jax
import jax.numpy as jnp
from jax import lax
from jax.sharding import PartitionSpec as P


def with_halo(value, sides, width):
    for axis, dim in sides:
        size, length = (lax.axis_size(axis), value.shape[dim])
        up = [(i, (i + 1) % size) for i in range(size)]
        down = [(j, i) for i, j in up]
        last = lax.slice_in_dim(value, length - width, length, axis=dim)
        first = lax.slice_in_dim(value, 0, width, axis=dim)
        before = lax.ppermute(last, axis, up)
        after = lax.ppermute(first, axis, down)
        value = jnp.concatenate([before, value, after], axis=dim)
    return value


def broadcast(block, axis, owner):
    block = jnp.where(lax.axis_index(axis) == owner, block, jnp.zeros_like(block))
    return lax.psum(block, axis)


def from_behind(value, axis, steps):
    count = lax.axis_size(axis)
    pairs = [(source, (source + steps) % count) for source in range(count)]
    return lax.ppermute(value, axis, pairs)


def band_conv(wide_band, weight):
    lon_len = wide_band.shape[2] - 4
    lat_len = wide_band.shape[3]
    padded = jnp.pad(wide_band, ((0, 0), (0, 0), (0, 0), (1, 1)))
    summed = jnp.zeros((weight.shape[1], wide_band.shape[1], lon_len, lat_len), jnp.float32)
    for shift_lon in range(5):
        for shift_lat in range(3):
            section = padded[:, :, shift_lon : shift_lon + lon_len, shift_lat : shift_lat + lat_len]
            summed = summed + jnp.einsum(
                "hc,cvxt->hvxt",
                weight[shift_lon * 3 + shift_lat],
                section,
                preferred_element_type=jnp.float32,
            )
    return summed


def upsample(extended, weight):
    lev_len = extended.shape[1] - 1
    lon_len = extended.shape[2] - 1
    lat_len = extended.shape[3] - 1
    tap_table = (((1, 0),), ((2, 0), (0, 1)))
    parity_parts = []
    for par_lev in range(2):
        for par_lon in range(2):
            for par_lat in range(2):
                summed = jnp.zeros((weight.shape[1], lev_len, lon_len, lat_len), jnp.float32)
                for tap_lev, off_lev in tap_table[par_lev]:
                    for tap_lon, off_lon in tap_table[par_lon]:
                        for tap_lat, off_lat in tap_table[par_lat]:
                            section = extended[
                                :,
                                off_lev : off_lev + lev_len,
                                off_lon : off_lon + lon_len,
                                off_lat : off_lat + lat_len,
                            ]
                            tap_weight = weight[tap_lev * 9 + tap_lon * 3 + tap_lat]
                            summed = summed + jnp.einsum(
                                "oc,cvxt->ovxt",
                                tap_weight,
                                section,
                                preferred_element_type=jnp.float32,
                            )
                parity_parts.append(summed)
    stacked = jnp.stack(parity_parts).reshape((2, 2, 2) + parity_parts[0].shape)
    reordered = jnp.transpose(stacked, (3, 4, 0, 5, 1, 6, 2))
    return reordered.reshape(weight.shape[1], 2 * lev_len, 2 * lon_len, 2 * lat_len)


def pad_ends(extended):
    return jnp.pad(extended, ((0, 0), (0, 1), (0, 0), (0, 1)))


def normalize(rows_in, values, gamma_rows, beta_rows):
    squares = values.astype(jnp.float32) * values.astype(jnp.float32)
    energy = beta_rows[:, None, None, None] + jnp.einsum(
        "ij,jvxt->ivxt", gamma_rows, squares, precision=lax.Precision.HIGHEST
    )
    return (rows_in.astype(jnp.float32) * jnp.sqrt(energy)).astype(jnp.bfloat16)


def local(
    symbols,
    hyper_mean,
    slice_order,
    hyper_weight,
    ctx_weight,
    ctx_bias,
    out_weight,
    gdn_beta,
    gdn_gamma,
    tconv_weight,
):
    slice_width, levels, lon_len, lat_len = symbols.shape
    channels = ctx_weight.shape[3]
    hyper_wide = with_halo(hyper_mean, (("lon", 2),), 2)
    start_pre = band_conv(hyper_wide, hyper_weight[0]) + ctx_bias[0][:, None, None, None]
    symbol_values = symbols.astype(jnp.float32)
    decoded = jnp.zeros((channels, levels, lon_len, lat_len), jnp.bfloat16)
    column = jnp.zeros((channels, levels, 1, lat_len), jnp.bfloat16)

    def decode(step_id, carry):
        pre_act, decoded, column = carry
        slice_id = slice_order[step_id]
        first_row = slice_id * slice_width
        hidden = jax.nn.gelu(pre_act, approximate=False).astype(jnp.bfloat16)
        slice_mean = jnp.einsum(
            "ch,hvxt->cvxt", out_weight[0], hidden, preferred_element_type=jnp.float32
        )
        candidate = (symbol_values + slice_mean).astype(jnp.bfloat16)
        decoded_rows = broadcast(candidate, "chan", slice_id)
        wide_band = with_halo(decoded_rows, (("lon", 2),), 2)
        weight_block = lax.dynamic_slice_in_dim(ctx_weight[0], first_row, slice_width, 2)
        pre_act = pre_act + band_conv(wide_band, weight_block)
        decoded = lax.dynamic_update_slice_in_dim(decoded, decoded_rows, first_row, 0)
        column = lax.dynamic_update_slice_in_dim(
            column, wide_band[:, :, lon_len + 2 : lon_len + 3], first_row, 0
        )
        return (pre_act, decoded, column)

    pre_act, decoded, column = lax.fori_loop(
        0, lax.axis_size("chan"), decode, (start_pre, decoded, column)
    )
    normed = normalize(decoded, decoded, gdn_gamma, gdn_beta)
    next_column = from_behind(normed[:, :, :1], "lon", -1)
    extended = jnp.concatenate([normed, next_column], axis=2)
    result = upsample(pad_ends(extended), tconv_weight)
    return result.astype(jnp.bfloat16)


def solution(mesh):
    placed = (
        P("chan", None, "lon", None),
        P("chan", None, "lon", None),
        P(),
        P("chan", None, None, None),
        P("chan", None, None, None),
        P("chan", None),
        P("chan", None, None),
        P(),
        P(),
        P(None, "chan", None),
    )
    return jax.shard_map(
        local, mesh=mesh, in_specs=placed, out_specs=P("chan", None, "lon", None), check_vma=False
    )
```

profile of v0, /device:TPU:225, one launch (start us, length us, event | category | flops | bytes accessed | tf_op | source)
XLA Modules:
  0.0 967.9 jit_solution(5462443687672508898)
XLA Ops:
  8.5 1.4 fusion.175
  10.0 5.3 collective-permute-done.3
  21.7 3.3 fusion.99
  25.0 1.3 broadcast_in_dim.4
  26.3 896.5 %while.17 = (s32[]{:T(128)}, f32[224,4,4,128]{3,0,2,1:T(8,128)}, bf16[320,4,4,128]{3,0,2,1:T(8,128)(2,1)}, s32[8]{0:T(128)S(1)}, bf16[1,15,224,320]{2,3,1,0:T(8,...) while((s32[]{:T(128)}, f32[224,4,4,128]{3,0,2,1:T(8,128)}, ...), condition=%wide.region_2.3_spmd, body=%wide.region_0.2_spmd.sunk | while | flops 626227200 | bytes 64425220 | solution.py:131
  27.5 6.2 fusion.339
  34.3 70.3 %all-reduce.5.cloned.1.call-done = bf16[40,4,4,128]{3,0,2,1:T(8,128)(2,1)} async-done(((bf16[40,4,4,128]{3,0,2,1:T(8,128)(2,1)}), bf16[40,4,4,128]{3,0,2,1:T(8,128)(2,1)}) %all-reduce.5.cloned.1.call-update) | async-done | bytes 163856 | tf_op jit(solution)/shard_map/while/body/eval_jaxpr/psum | solution.py:22
  105.6 7.2 collective-permute-start
  112.9 1.3 fusion.348
  115.1 5.2 collective-permute-done.1
  128.8 1.2 fusion.350
  133.5 1.2 fusion.344
  135.9 4.6 add_add_fusion.2
  141.7 6.2 fusion.339
  148.5 67.9 %all-reduce.5.cloned.1.call-done = bf16[40,4,4,128]{3,0,2,1:T(8,128)(2,1)} async-done(((bf16[40,4,4,128]{3,0,2,1:T(8,128)(2,1)}), bf16[40,4,4,128]{3,0,2,1:T(8,128)(2,1)}) %all-reduce.5.cloned.1.call-update) | async-done | bytes 163856 | tf_op jit(solution)/shard_map/while/body/eval_jaxpr/psum | solution.py:22
  217.4 7.2 collective-permute-start
  224.6 1.3 fusion.348
  226.9 5.2 collective-permute-done.1
  240.5 1.2 fusion.350
  245.3 1.2 fusion.344
  247.6 4.6 add_add_fusion.2
  253.4 6.2 fusion.339
  260.2 67.9 %all-reduce.5.cloned.1.call-done = bf16[40,4,4,128]{3,0,2,1:T(8,128)(2,1)} async-done(((bf16[40,4,4,128]{3,0,2,1:T(8,128)(2,1)}), bf16[40,4,4,128]{3,0,2,1:T(8,128)(2,1)}) %all-reduce.5.cloned.1.call-update) | async-done | bytes 163856 | tf_op jit(solution)/shard_map/while/body/eval_jaxpr/psum | solution.py:22
  329.1 7.2 collective-permute-start
  336.3 1.3 fusion.348
  338.6 5.2 collective-permute-done.1
  352.2 1.2 fusion.350
  359.3 4.6 add_add_fusion.2
  365.1 6.2 fusion.339
  371.9 67.9 %all-reduce.5.cloned.1.call-done = bf16[40,4,4,128]{3,0,2,1:T(8,128)(2,1)} async-done(((bf16[40,4,4,128]{3,0,2,1:T(8,128)(2,1)}), bf16[40,4,4,128]{3,0,2,1:T(8,128)(2,1)}) %all-reduce.5.cloned.1.call-update) | async-done | bytes 163856 | tf_op jit(solution)/shard_map/while/body/eval_jaxpr/psum | solution.py:22
  440.8 7.2 collective-permute-start
  448.1 1.4 fusion.348
  450.3 5.2 collective-permute-done.1
  471.1 4.6 add_add_fusion.2
  476.8 6.2 fusion.339
  483.7 68.0 %all-reduce.5.cloned.1.call-done = bf16[40,4,4,128]{3,0,2,1:T(8,128)(2,1)} async-done(((bf16[40,4,4,128]{3,0,2,1:T(8,128)(2,1)}), bf16[40,4,4,128]{3,0,2,1:T(8,128)(2,1)}) %all-reduce.5.cloned.1.call-update) | async-done | bytes 163856 | tf_op jit(solution)/shard_map/while/body/eval_jaxpr/psum | solution.py:22
  552.7 7.2 collective-permute-start
  559.9 1.3 fusion.348
  562.2 5.2 collective-permute-done.1
  582.9 4.6 add_add_fusion.2
  588.7 6.2 fusion.339
  595.5 67.9 %all-reduce.5.cloned.1.call-done = bf16[40,4,4,128]{3,0,2,1:T(8,128)(2,1)} async-done(((bf16[40,4,4,128]{3,0,2,1:T(8,128)(2,1)}), bf16[40,4,4,128]{3,0,2,1:T(8,128)(2,1)}) %all-reduce.5.cloned.1.call-update) | async-done | bytes 163856 | tf_op jit(solution)/shard_map/while/body/eval_jaxpr/psum | solution.py:22
  664.4 7.2 collective-permute-start
  671.6 1.3 fusion.348
  673.9 5.2 collective-permute-done.1
  692.2 1.2 fusion.344
  694.6 4.6 add_add_fusion.2
  700.4 6.2 fusion.339
  707.2 67.9 %all-reduce.5.cloned.1.call-done = bf16[40,4,4,128]{3,0,2,1:T(8,128)(2,1)} async-done(((bf16[40,4,4,128]{3,0,2,1:T(8,128)(2,1)}), bf16[40,4,4,128]{3,0,2,1:T(8,128)(2,1)}) %all-reduce.5.cloned.1.call-update) | async-done | bytes 163856 | tf_op jit(solution)/shard_map/while/body/eval_jaxpr/psum | solution.py:22
  776.1 7.2 collective-permute-start
  783.3 1.4 fusion.348
  785.6 5.2 collective-permute-done.1
  799.3 1.2 fusion.350
  806.3 4.6 add_add_fusion.2
  812.1 6.2 fusion.339
  819.0 67.9 %all-reduce.5.cloned.1.call-done = bf16[40,4,4,128]{3,0,2,1:T(8,128)(2,1)} async-done(((bf16[40,4,4,128]{3,0,2,1:T(8,128)(2,1)}), bf16[40,4,4,128]{3,0,2,1:T(8,128)(2,1)}) %all-reduce.5.cloned.1.call-update) | async-done | bytes 163856 | tf_op jit(solution)/shard_map/while/body/eval_jaxpr/psum | solution.py:22
  887.9 7.2 collective-permute-start
  895.1 1.3 fusion.348
  897.3 5.2 collective-permute-done.1
  918.1 4.6 add_add_fusion.2
  922.7 7.1 fusion.98
  932.5 9.5 collective-permute-done.4
  949.4 7.2 copy.26
  956.6 4.4 copy.27
  (264 shorter events, 153.6 us)
Async XLA Ops:
  6.5 916.2 %copy-start = (f32[320,320]{1,0:T(8,128)S(1)}, f32[320,320]{1,0:T(8,128)}, u32[]{:S(2)}) copy-start(f32[320,320]{1,0:T(8,128)} %param.20) | copy-start | bytes 1228804
  6.5 3.3 copy-start.3
  7.6 8.0 copy-start.4
  7.6 2.3 collective-permute-start.2
  7.8 7.5 collective-permute-start.3
  18.8 0.9 copy-start.2
  20.8 0.9 copy-start.6
  21.7 4.6 copy-start.7
  21.7 4.6 copy-start.9
  26.3 896.5 %copy-start.8 = (f32[320]{0:T(512)S(1)}, f32[320]{0:T(512)}, u32[]{:S(2)}) copy-start(f32[320]{0:T(512)} %param.19) | copy-start | bytes 3844
  26.3 78.4 %all-reduce.5.cloned.1.call-start = ((), (), s32[]{:S(2)}) async-start(), calls=%async_computation | async-start | bytes 327680 | tf_op jit(solution)/shard_map/while/body/eval_jaxpr/psum | solution.py:22
  104.7 9.7 %copy-start.1 = (bf16[40,4,4,128]{3,0,2,1:T(8,128)(2,1)S(1)}, bf16[40,4,4,128]{3,0,2,1:T(8,128)(2,1)}, u32[]{:S(2)}) copy-start(bf16[40,4,4,128]{3,0,2,1:T(8,128)(2,1)} %all-reduce.5.cloned.1.call-done) | copy-start | bytes 491524 | tf_op jit(solution)/shard_map/while
  105.6 8.7 collective-permute-start
  112.9 7.5 collective-permute-start.1
  140.5 75.9 %all-reduce.5.cloned.1.call-start = ((), (), s32[]{:S(2)}) async-start(), calls=%async_computation | async-start | bytes 327680 | tf_op jit(solution)/shard_map/while/body/eval_jaxpr/psum | solution.py:22
  216.4 9.7 %copy-start.1 = (bf16[40,4,4,128]{3,0,2,1:T(8,128)(2,1)S(1)}, bf16[40,4,4,128]{3,0,2,1:T(8,128)(2,1)}, u32[]{:S(2)}) copy-start(bf16[40,4,4,128]{3,0,2,1:T(8,128)(2,1)} %all-reduce.5.cloned.1.call-done) | copy-start | bytes 491524 | tf_op jit(solution)/shard_map/while
  217.4 8.7 collective-permute-start
  224.6 7.5 collective-permute-start.1
  252.3 75.8 %all-reduce.5.cloned.1.call-start = ((), (), s32[]{:S(2)}) async-start(), calls=%async_computation | async-start | bytes 327680 | tf_op jit(solution)/shard_map/while/body/eval_jaxpr/psum | solution.py:22
  328.1 9.7 %copy-start.1 = (bf16[40,4,4,128]{3,0,2,1:T(8,128)(2,1)S(1)}, bf16[40,4,4,128]{3,0,2,1:T(8,128)(2,1)}, u32[]{:S(2)}) copy-start(bf16[40,4,4,128]{3,0,2,1:T(8,128)(2,1)} %all-reduce.5.cloned.1.call-done) | copy-start | bytes 491524 | tf_op jit(solution)/shard_map/while
  329.1 8.7 collective-permute-start
  336.3 7.5 collective-permute-start.1
  363.9 75.9 %all-reduce.5.cloned.1.call-start = ((), (), s32[]{:S(2)}) async-start(), calls=%async_computation | async-start | bytes 327680 | tf_op jit(solution)/shard_map/while/body/eval_jaxpr/psum | solution.py:22
  439.9 9.7 %copy-start.1 = (bf16[40,4,4,128]{3,0,2,1:T(8,128)(2,1)S(1)}, bf16[40,4,4,128]{3,0,2,1:T(8,128)(2,1)}, u32[]{:S(2)}) copy-start(bf16[40,4,4,128]{3,0,2,1:T(8,128)(2,1)} %all-reduce.5.cloned.1.call-done) | copy-start | bytes 491524 | tf_op jit(solution)/shard_map/while
  440.8 8.7 collective-permute-start
  448.0 7.5 collective-permute-start.1
  475.7 76.0 %all-reduce.5.cloned.1.call-start = ((), (), s32[]{:S(2)}) async-start(), calls=%async_computation | async-start | bytes 327680 | tf_op jit(solution)/shard_map/while/body/eval_jaxpr/psum | solution.py:22
  551.7 9.7 %copy-start.1 = (bf16[40,4,4,128]{3,0,2,1:T(8,128)(2,1)S(1)}, bf16[40,4,4,128]{3,0,2,1:T(8,128)(2,1)}, u32[]{:S(2)}) copy-start(bf16[40,4,4,128]{3,0,2,1:T(8,128)(2,1)} %all-reduce.5.cloned.1.call-done) | copy-start | bytes 491524 | tf_op jit(solution)/shard_map/while
  552.7 8.7 collective-permute-start
  559.9 7.5 collective-permute-start.1
  587.5 75.9 %all-reduce.5.cloned.1.call-start = ((), (), s32[]{:S(2)}) async-start(), calls=%async_computation | async-start | bytes 327680 | tf_op jit(solution)/shard_map/while/body/eval_jaxpr/psum | solution.py:22
  663.4 9.7 %copy-start.1 = (bf16[40,4,4,128]{3,0,2,1:T(8,128)(2,1)S(1)}, bf16[40,4,4,128]{3,0,2,1:T(8,128)(2,1)}, u32[]{:S(2)}) copy-start(bf16[40,4,4,128]{3,0,2,1:T(8,128)(2,1)} %all-reduce.5.cloned.1.call-done) | copy-start | bytes 491524 | tf_op jit(solution)/shard_map/while
  664.4 8.7 collective-permute-start
  671.6 7.5 collective-permute-start.1
  699.2 75.9 %all-reduce.5.cloned.1.call-start = ((), (), s32[]{:S(2)}) async-start(), calls=%async_computation | async-start | bytes 327680 | tf_op jit(solution)/shard_map/while/body/eval_jaxpr/psum | solution.py:22
  775.1 9.7 %copy-start.1 = (bf16[40,4,4,128]{3,0,2,1:T(8,128)(2,1)S(1)}, bf16[40,4,4,128]{3,0,2,1:T(8,128)(2,1)}, u32[]{:S(2)}) copy-start(bf16[40,4,4,128]{3,0,2,1:T(8,128)(2,1)} %all-reduce.5.cloned.1.call-done) | copy-start | bytes 491524 | tf_op jit(solution)/shard_map/while
  776.1 8.7 collective-permute-start
  783.3 7.5 collective-permute-start.1
  811.0 75.9 %all-reduce.5.cloned.1.call-start = ((), (), s32[]{:S(2)}) async-start(), calls=%async_computation | async-start | bytes 327680 | tf_op jit(solution)/shard_map/while/body/eval_jaxpr/psum | solution.py:22
  886.9 9.7 %copy-start.1 = (bf16[40,4,4,128]{3,0,2,1:T(8,128)(2,1)S(1)}, bf16[40,4,4,128]{3,0,2,1:T(8,128)(2,1)}, u32[]{:S(2)}) copy-start(bf16[40,4,4,128]{3,0,2,1:T(8,128)(2,1)} %all-reduce.5.cloned.1.call-done) | copy-start | bytes 491524 | tf_op jit(solution)/shard_map/while
  887.9 8.7 collective-permute-start
  895.1 7.5 collective-permute-start.1
  922.7 7.1 copy-start.5
  931.6 10.5 %collective-permute-start.4 = (bf16[320,4,1,128]{3,0,2,1:T(8,128)(2,1)S(1)}, bf16[320,4,1,128]{3,0,2,1:T(8,128)(2,1)S(1)}, u32[]{:S(2)}, u32[]{:S(2)}) collective-permute-start(bf16[320,4,1,128]{3,0,2,1:T(8,128)(2,1)S(1)} %slice.676), channel_id=1, source_target_pairs={{0,31},{1,0},{2,1},{3,2},{4,3},{5,4},{6,5},{7,6},{8,7},{9,8},{10,9... | collective-permute-start | bytes 983048 | tf_op jit(solution)/shard_map/ppermute | solution.py:28
Sparse Core Ops, SparseCore 0:
  33.9 70.7 all-reduce.4
  148.0 68.3 all-reduce.4
  259.8 68.2 all-reduce.4
  371.5 68.3 all-reduce.4
  483.2 68.3 all-reduce.4
  595.1 68.2 all-reduce.4
  706.8 68.3 all-reduce.4
  818.5 68.2 all-reduce.4
where the time goes:
time: 975 us; the launch traced here: 968 us
  waiting for transfers between devices  603 us (62%)
  matrix products  246 us (25%)
  starting transfers between devices  58.9 us (6%)
  local copies, waits for them, and re-layouts  33.1 us (3%)
  between operations  13.7 us (1%)
    psum x8, waiting for transfers between devices, broadcast(): return lax.psum(block, axis)  546 us
    dot_general x135, matrix products, band_conv(): jnp.einsum('hc,cvxt->hvxt', weight[shift_lon * 3 + shift_lat], section, p...  180 us
    ppermute x9, starting transfers between devices, with_halo(): before = lax.ppermute(last, axis, up)  57.8 us
    dot_general x8, matrix products, decode(): jnp.einsum('ch,hvxt->cvxt', out_weight[0], hidden, preferred_element_type...  50 us
    ppermute x9, waiting for transfers between devices, with_halo(): after = lax.ppermute(first, axis, down)  47 us
  transfers between devices with their start and end apart: 27, of which 26 were waited for; matrix products, arithmetic and copies ran while one was open for 2% of the time, Pallas kernels for 0%

commit v1 on v0

--- a/solution.py
+++ b/solution.py
@@ -19,7 +19,7 @@
 
 def broadcast(block, axis, owner):
     block = jnp.where(lax.axis_index(axis) == owner, block, jnp.zeros_like(block))
-    return lax.psum(block, axis)
+    return jnp.sum(lax.all_gather(block, axis_name=axis), axis=0)
 
 
 def from_behind(value, axis, steps):

time: 975 us -> 699 us (0.72)
  waiting for transfers between devices: 603 us -> 303 us
  matrix products: 246 us -> 258 us
  other arithmetic: 3.04 us -> 15 us
    psum x8 -> x0, waiting for transfers between devices: 546 us -> none  [broadcast(): return lax.psum(block, axis)]
    all_gather x0 -> x8, waiting for transfers between devices: none -> 287 us  [broadcast(): return jnp.sum(lax.all_gather(block, axis_name=axis), axis=0)]
    ppermute x9, starting transfers between devices: 0.67 us -> 51.4 us  [with_halo(): after = lax.ppermute(first, axis, down)]
    ppermute x9, starting transfers between devices: 57.8 us -> 14.1 us  [with_halo(): before = lax.ppermute(last, axis, up)]
    ppermute x9, waiting for transfers between devices: 47 us -> 6.53 us  [with_halo(): after = lax.ppermute(first, axis, down)]
    reduce_sum x0 -> x8, other arithmetic: none -> 12 us  [broadcast(): return jnp.sum(lax.all_gather(block, axis_name=axis), axis=0)]
    dot_general x135, matrix products: 180 us -> 191 us  [band_conv(): jnp.einsum('hc,cvxt->hvxt', weight[shift_lon * 3 + shift_lat], section, p...]
  transfers between devices with their start and end apart: 27 -> 27, of which waited for: 26 -> 18; matrix products, arithmetic and copies ran while one was open for 2% -> 2% of each run, Pallas kernels for 0% -> 0%
where the time goes in v1:
time: 699 us; the launch traced here: 692 us
  waiting for transfers between devices  303 us (43%)
  matrix products  258 us (37%)
  starting transfers between devices  66.1 us (9%)
  local copies, waits for them, and re-layouts  25.4 us (4%)
  other arithmetic  15 us (2%)
  between operations  13.7 us (2%)
  loops' own time  10.8 us (2%)
    all_gather x8, waiting for transfers between devices, broadcast(): return jnp.sum(lax.all_gather(block, axis_name=axis), axis=0)  287 us
    dot_general x135, matrix products, band_conv(): jnp.einsum('hc,cvxt->hvxt', weight[shift_lon * 3 + shift_lat], section, p...  191 us
    ppermute x9, starting transfers between devices, with_halo(): after = lax.ppermute(first, axis, down)  51.4 us
    dot_general x8, matrix products, decode(): jnp.einsum('ch,hvxt->cvxt', out_weight[0], hidden, preferred_element_type...  50 us
    ppermute x9, starting transfers between devices, with_halo(): before = lax.ppermute(last, axis, up)  14.1 us
  transfers between devices with their start and end apart: 27, of which 18 were waited for; matrix products, arithmetic and copies ran while one was open for 2% of the time, Pallas kernels for 0%

profile of v1, /device:TPU:225, one launch (start us, length us, event | category | flops | bytes accessed | tf_op | source)
XLA Modules:
  0.0 691.9 jit_solution(3239844957052482611)
XLA Ops:
  8.5 1.4 fusion.181
  10.0 5.3 collective-permute-done.3
  21.7 3.3 fusion.105
  26.3 620.4 %while.18 = (s32[]{:T(128)}, f32[224,4,4,128]{3,0,2,1:T(8,128)}, bf16[320,4,4,128]{3,0,2,1:T(8,128)(2,1)}, s32[8]{0:T(128)S(1)}, bf16[1,15,224,320]{2,3,1,0:T(8,...) while((s32[]{:T(128)}, f32[224,4,4,128]{3,0,2,1:T(8,128)}, ...), condition=%wide.region_2.3_spmd, body=%wide.region_0.2_spmd.sunk | while | flops 628029440 | bytes 68357352 | solution.py:131
  27.7 6.2 fusion.341
  34.6 34.7 %all-gather.5.cloned.1.call-done = bf16[320,4,4,128]{3,0,2,1:T(8,128)(2,1)} async-done(((bf16[40,4,4,128]{3,0,2,1:T(8,128)(2,1)}), bf16[320,4,4,128]{3,0,2,1:T(8,128)(2,1)}) %all-gather.5.cloned.1.call-update) | async-done | bytes 1310736 | tf_op jit(solution)/shard_map/while/body/eval_jaxpr/all_gather | solution.py:22
  69.3 1.5 reduce_sum.15
  70.8 6.4 collective-permute-start
  77.2 1.7 collective-permute-start.1
  95.3 2.4 fusion.343
  97.7 5.1 add_add_fusion.2
  104.1 6.2 fusion.341
  111.0 36.0 %all-gather.5.cloned.1.call-done = bf16[320,4,4,128]{3,0,2,1:T(8,128)(2,1)} async-done(((bf16[40,4,4,128]{3,0,2,1:T(8,128)(2,1)}), bf16[320,4,4,128]{3,0,2,1:T(8,128)(2,1)}) %all-gather.5.cloned.1.call-update) | async-done | bytes 1310736 | tf_op jit(solution)/shard_map/while/body/eval_jaxpr/all_gather | solution.py:22
  147.0 1.5 reduce_sum.15
  148.5 6.4 collective-permute-start
  154.9 1.7 collective-permute-start.1
  173.0 2.4 fusion.343
  175.4 5.1 add_add_fusion.2
  181.8 6.2 fusion.341
  188.7 36.0 %all-gather.5.cloned.1.call-done = bf16[320,4,4,128]{3,0,2,1:T(8,128)(2,1)} async-done(((bf16[40,4,4,128]{3,0,2,1:T(8,128)(2,1)}), bf16[320,4,4,128]{3,0,2,1:T(8,128)(2,1)}) %all-gather.5.cloned.1.call-update) | async-done | bytes 1310736 | tf_op jit(solution)/shard_map/while/body/eval_jaxpr/all_gather | solution.py:22
  224.7 1.5 reduce_sum.15
  226.2 6.4 collective-permute-start
  232.6 1.7 collective-permute-start.1
  250.7 2.4 fusion.343
  253.1 5.1 add_add_fusion.2
  259.5 6.2 fusion.341
  266.4 36.0 %all-gather.5.cloned.1.call-done = bf16[320,4,4,128]{3,0,2,1:T(8,128)(2,1)} async-done(((bf16[40,4,4,128]{3,0,2,1:T(8,128)(2,1)}), bf16[320,4,4,128]{3,0,2,1:T(8,128)(2,1)}) %all-gather.5.cloned.1.call-update) | async-done | bytes 1310736 | tf_op jit(solution)/shard_map/while/body/eval_jaxpr/all_gather | solution.py:22
  302.4 1.5 reduce_sum.15
  303.9 6.4 collective-permute-start
  310.3 1.7 collective-permute-start.1
  328.4 2.4 fusion.343
  330.8 5.1 add_add_fusion.2
  337.2 6.2 fusion.341
  344.1 36.0 %all-gather.5.cloned.1.call-done = bf16[320,4,4,128]{3,0,2,1:T(8,128)(2,1)} async-done(((bf16[40,4,4,128]{3,0,2,1:T(8,128)(2,1)}), bf16[320,4,4,128]{3,0,2,1:T(8,128)(2,1)}) %all-gather.5.cloned.1.call-update) | async-done | bytes 1310736 | tf_op jit(solution)/shard_map/while/body/eval_jaxpr/all_gather | solution.py:22
  380.1 1.5 reduce_sum.15
  381.6 6.4 collective-permute-start
  388.0 1.7 collective-permute-start.1
  406.1 2.4 fusion.343
  408.5 5.1 add_add_fusion.2
  414.9 6.2 fusion.341
  421.8 36.0 %all-gather.5.cloned.1.call-done = bf16[320,4,4,128]{3,0,2,1:T(8,128)(2,1)} async-done(((bf16[40,4,4,128]{3,0,2,1:T(8,128)(2,1)}), bf16[320,4,4,128]{3,0,2,1:T(8,128)(2,1)}) %all-gather.5.cloned.1.call-update) | async-done | bytes 1310736 | tf_op jit(solution)/shard_map/while/body/eval_jaxpr/all_gather | solution.py:22
  457.8 1.5 reduce_sum.15
  459.3 6.4 collective-permute-start
  465.7 1.7 collective-permute-start.1
  483.8 2.4 fusion.343
  486.2 5.1 add_add_fusion.2
  492.6 6.2 fusion.341
  499.5 36.0 %all-gather.5.cloned.1.call-done = bf16[320,4,4,128]{3,0,2,1:T(8,128)(2,1)} async-done(((bf16[40,4,4,128]{3,0,2,1:T(8,128)(2,1)}), bf16[320,4,4,128]{3,0,2,1:T(8,128)(2,1)}) %all-gather.5.cloned.1.call-update) | async-done | bytes 1310736 | tf_op jit(solution)/shard_map/while/body/eval_jaxpr/all_gather | solution.py:22
  535.5 1.5 reduce_sum.15
  537.0 6.4 collective-permute-start
  543.4 1.7 collective-permute-start.1
  561.5 2.4 fusion.343
  563.9 5.1 add_add_fusion.2
  570.3 6.2 fusion.341
  577.2 36.0 %all-gather.5.cloned.1.call-done = bf16[320,4,4,128]{3,0,2,1:T(8,128)(2,1)} async-done(((bf16[40,4,4,128]{3,0,2,1:T(8,128)(2,1)}), bf16[320,4,4,128]{3,0,2,1:T(8,128)(2,1)}) %all-gather.5.cloned.1.call-update) | async-done | bytes 1310736 | tf_op jit(solution)/shard_map/while/body/eval_jaxpr/all_gather | solution.py:22
  613.2 1.5 reduce_sum.15
  614.7 6.4 collective-permute-start
  621.1 1.7 collective-permute-start.1
  639.2 2.4 fusion.343
  641.6 5.1 add_add_fusion.2
  646.7 7.1 %fusion.104 = bf16[320,4,4,128]{3,0,2,1:T(8,128)(2,1)S(1)} fusion(bf16[320,4,4,128]{3,0,2,1:T(8,128)(2,1)} %get-tuple-element.201, f32[320]{0:T(512)S(1)} %copy-done.7, f32[320,320]{1,0:T(8,128)S(1)} %copy-done), kind=kOutput, calls=%fused_computation.142 | convolution fusion | flops 2520514560 | bytes 3032320 | tf_op jit(solution)/shard_map/ij,jvxt->ivxt/dot_general | solution.py:86
  656.6 9.5 %collective-permute-done.4 = bf16[320,4,1,128]{3,0,2,1:T(8,128)(2,1)S(1)} collective-permute-done((bf16[320,4,1,128]{3,0,2,1:T(8,128)(2,1)S(1)}, bf16[320,4,1,128]{3,0,2,1:T(8,128)(2,1)S(1)}, u32[]{:S(2)}, u32[]{:S(2)}) %collective-permute-start.4) | collective-permute-done | bytes 327712 | tf_op jit(solution)/shard_map/ppermute | solution.py:28
  673.5 7.2 %copy.26 = bf16[2,2,2,8,4,4,128]{3,2,6,1,5,0,4:T(2,128)(2,1)} copy(bf16[2,2,2,8,4,4,128]{6,3,5,4,2,1,0:T(8,128)(2,1)S(1)} %bitcast.563) | data formatting | bytes 524288 | tf_op jit(solution)/shard_map/convert_element_type | solution.py:138
  680.7 4.4 copy.27
  (240 shorter events, 155.8 us)
Async XLA Ops:
  6.5 640.1 %copy-start = (f32[320,320]{1,0:T(8,128)S(1)}, f32[320,320]{1,0:T(8,128)}, u32[]{:S(2)}) copy-start(f32[320,320]{1,0:T(8,128)} %param.20) | copy-start | bytes 1228804
  6.5 3.3 copy-start.2
  7.6 8.0 %copy-start.3 = (bf16[1,15,224,40]{2,3,1,0:T(8,128)(2,1)S(1)}, bf16[1,15,224,40]{2,3,1,0:T(8,128)(2,1)}, u32[]{:S(2)}) copy-start(bf16[1,15,224,40]{2,3,1,0:T(8,128)(2,1)} %param.15) | copy-start | bytes 806404
  7.6 2.3 collective-permute-start.2
  7.8 7.5 %collective-permute-start.3 = (bf16[40,4,2,128]{3,0,2,1:T(8,128)(2,1)S(1)}, bf16[40,4,2,128]{3,0,2,1:T(8,128)(2,1)S(1)}, u32[]{:S(2)}, u32[]{:S(2)}) collective-permute-start(bf16[40,4,2,128]{3,0,2,1:T(8,128)(2,1)S(1)} %get-tuple-element.221), channel_id=1, source_target_pairs={{1,0},{2,1},{3,2},{4,3},{5,4},{6,5},{7,6},{8,7},{9,8},{10,9},{11,1... | collective-permute-start | bytes 245768 | tf_op jit(solution)/shard_map/ppermute | solution.py:15
  18.8 0.9 copy-start.1
  20.8 0.9 copy-start.5
  21.7 4.6 copy-start.6
  21.7 4.6 copy-start.8
  26.3 620.4 %copy-start.7 = (f32[320]{0:T(512)S(1)}, f32[320]{0:T(512)}, u32[]{:S(2)}) copy-start(f32[320]{0:T(512)} %param.19) | copy-start | bytes 3844
  26.3 43.0 %all-gather.5.cloned.1.call-start = ((), (), s32[]{:S(2)}) async-start(), calls=%async_computation | async-start | bytes 1474560 | tf_op jit(solution)/shard_map/while/body/eval_jaxpr/all_gather | solution.py:22
  70.8 10.1 %collective-permute-start = (bf16[40,4,2,128]{3,0,2,1:T(8,128)(2,1)S(1)}, bf16[40,4,2,128]{3,0,2,1:T(8,128)(2,1)S(1)}, u32[]{:S(2)}, u32[]{:S(2)}) collective-permute-start(bf16[40,4,2,128]{3,0,2,1:T(8,128)(2,1)S(1)} %get-tuple-element.267), channel_id=1, source_target_pairs={{1,0},{2,1},{3,2},{4,3},{5,4},{6,5},{7,6},{8,7},{9,8},{10,9},{11,1... | collective-permute-start | bytes 245768 | tf_op jit(solution)/shard_map/while/body/eval_jaxpr/ppermute | solution.py:15
  77.2 3.8 collective-permute-start.1
  102.8 44.2 %all-gather.5.cloned.1.call-start = ((), (), s32[]{:S(2)}) async-start(), calls=%async_computation | async-start | bytes 1474560 | tf_op jit(solution)/shard_map/while/body/eval_jaxpr/all_gather | solution.py:22
  148.5 10.1 %collective-permute-start = (bf16[40,4,2,128]{3,0,2,1:T(8,128)(2,1)S(1)}, bf16[40,4,2,128]{3,0,2,1:T(8,128)(2,1)S(1)}, u32[]{:S(2)}, u32[]{:S(2)}) collective-permute-start(bf16[40,4,2,128]{3,0,2,1:T(8,128)(2,1)S(1)} %get-tuple-element.267), channel_id=1, source_target_pairs={{1,0},{2,1},{3,2},{4,3},{5,4},{6,5},{7,6},{8,7},{9,8},{10,9},{11,1... | collective-permute-start | bytes 245768 | tf_op jit(solution)/shard_map/while/body/eval_jaxpr/ppermute | solution.py:15
  154.9 3.8 collective-permute-start.1
  180.5 44.2 %all-gather.5.cloned.1.call-start = ((), (), s32[]{:S(2)}) async-start(), calls=%async_computation | async-start | bytes 1474560 | tf_op jit(solution)/shard_map/while/body/eval_jaxpr/all_gather | solution.py:22
  226.2 10.1 %collective-permute-start = (bf16[40,4,2,128]{3,0,2,1:T(8,128)(2,1)S(1)}, bf16[40,4,2,128]{3,0,2,1:T(8,128)(2,1)S(1)}, u32[]{:S(2)}, u32[]{:S(2)}) collective-permute-start(bf16[40,4,2,128]{3,0,2,1:T(8,128)(2,1)S(1)} %get-tuple-element.267), channel_id=1, source_target_pairs={{1,0},{2,1},{3,2},{4,3},{5,4},{6,5},{7,6},{8,7},{9,8},{10,9},{11,1... | collective-permute-start | bytes 245768 | tf_op jit(solution)/shard_map/while/body/eval_jaxpr/ppermute | solution.py:15
  232.6 3.8 collective-permute-start.1
  258.2 44.2 %all-gather.5.cloned.1.call-start = ((), (), s32[]{:S(2)}) async-start(), calls=%async_computation | async-start | bytes 1474560 | tf_op jit(solution)/shard_map/while/body/eval_jaxpr/all_gather | solution.py:22
  303.9 10.1 %collective-permute-start = (bf16[40,4,2,128]{3,0,2,1:T(8,128)(2,1)S(1)}, bf16[40,4,2,128]{3,0,2,1:T(8,128)(2,1)S(1)}, u32[]{:S(2)}, u32[]{:S(2)}) collective-permute-start(bf16[40,4,2,128]{3,0,2,1:T(8,128)(2,1)S(1)} %get-tuple-element.267), channel_id=1, source_target_pairs={{1,0},{2,1},{3,2},{4,3},{5,4},{6,5},{7,6},{8,7},{9,8},{10,9},{11,1... | collective-permute-start | bytes 245768 | tf_op jit(solution)/shard_map/while/body/eval_jaxpr/ppermute | solution.py:15
  310.3 3.8 collective-permute-start.1
  335.9 44.2 %all-gather.5.cloned.1.call-start = ((), (), s32[]{:S(2)}) async-start(), calls=%async_computation | async-start | bytes 1474560 | tf_op jit(solution)/shard_map/while/body/eval_jaxpr/all_gather | solution.py:22
  381.6 10.1 %collective-permute-start = (bf16[40,4,2,128]{3,0,2,1:T(8,128)(2,1)S(1)}, bf16[40,4,2,128]{3,0,2,1:T(8,128)(2,1)S(1)}, u32[]{:S(2)}, u32[]{:S(2)}) collective-permute-start(bf16[40,4,2,128]{3,0,2,1:T(8,128)(2,1)S(1)} %get-tuple-element.267), channel_id=1, source_target_pairs={{1,0},{2,1},{3,2},{4,3},{5,4},{6,5},{7,6},{8,7},{9,8},{10,9},{11,1... | collective-permute-start | bytes 245768 | tf_op jit(solution)/shard_map/while/body/eval_jaxpr/ppermute | solution.py:15
  388.0 3.8 collective-permute-start.1
  413.6 44.2 %all-gather.5.cloned.1.call-start = ((), (), s32[]{:S(2)}) async-start(), calls=%async_computation | async-start | bytes 1474560 | tf_op jit(solution)/shard_map/while/body/eval_jaxpr/all_gather | solution.py:22
  459.3 10.1 %collective-permute-start = (bf16[40,4,2,128]{3,0,2,1:T(8,128)(2,1)S(1)}, bf16[40,4,2,128]{3,0,2,1:T(8,128)(2,1)S(1)}, u32[]{:S(2)}, u32[]{:S(2)}) collective-permute-start(bf16[40,4,2,128]{3,0,2,1:T(8,128)(2,1)S(1)} %get-tuple-element.267), channel_id=1, source_target_pairs={{1,0},{2,1},{3,2},{4,3},{5,4},{6,5},{7,6},{8,7},{9,8},{10,9},{11,1... | collective-permute-start | bytes 245768 | tf_op jit(solution)/shard_map/while/body/eval_jaxpr/ppermute | solution.py:15
  465.7 3.8 collective-permute-start.1
  491.3 44.2 %all-gather.5.cloned.1.call-start = ((), (), s32[]{:S(2)}) async-start(), calls=%async_computation | async-start | bytes 1474560 | tf_op jit(solution)/shard_map/while/body/eval_jaxpr/all_gather | solution.py:22
  537.0 10.1 %collective-permute-start = (bf16[40,4,2,128]{3,0,2,1:T(8,128)(2,1)S(1)}, bf16[40,4,2,128]{3,0,2,1:T(8,128)(2,1)S(1)}, u32[]{:S(2)}, u32[]{:S(2)}) collective-permute-start(bf16[40,4,2,128]{3,0,2,1:T(8,128)(2,1)S(1)} %get-tuple-element.267), channel_id=1, source_target_pairs={{1,0},{2,1},{3,2},{4,3},{5,4},{6,5},{7,6},{8,7},{9,8},{10,9},{11,1... | collective-permute-start | bytes 245768 | tf_op jit(solution)/shard_map/while/body/eval_jaxpr/ppermute | solution.py:15
  543.4 3.8 collective-permute-start.1
  569.0 44.2 %all-gather.5.cloned.1.call-start = ((), (), s32[]{:S(2)}) async-start(), calls=%async_computation | async-start | bytes 1474560 | tf_op jit(solution)/shard_map/while/body/eval_jaxpr/all_gather | solution.py:22
  614.7 10.1 %collective-permute-start = (bf16[40,4,2,128]{3,0,2,1:T(8,128)(2,1)S(1)}, bf16[40,4,2,128]{3,0,2,1:T(8,128)(2,1)S(1)}, u32[]{:S(2)}, u32[]{:S(2)}) collective-permute-start(bf16[40,4,2,128]{3,0,2,1:T(8,128)(2,1)S(1)} %get-tuple-element.267), channel_id=1, source_target_pairs={{1,0},{2,1},{3,2},{4,3},{5,4},{6,5},{7,6},{8,7},{9,8},{10,9},{11,1... | collective-permute-start | bytes 245768 | tf_op jit(solution)/shard_map/while/body/eval_jaxpr/ppermute | solution.py:15
  621.1 3.8 collective-permute-start.1
  646.7 7.1 %copy-start.4 = (bf16[27,8,320]{2,1,0:T(8,128)(2,1)S(1)}, bf16[27,8,320]{2,1,0:T(8,128)(2,1)}, u32[]{:S(2)}) copy-start(bf16[27,8,320]{2,1,0:T(8,128)(2,1)} %param.21) | copy-start | bytes 414724
  655.6 10.5 %collective-permute-start.4 = (bf16[320,4,1,128]{3,0,2,1:T(8,128)(2,1)S(1)}, bf16[320,4,1,128]{3,0,2,1:T(8,128)(2,1)S(1)}, u32[]{:S(2)}, u32[]{:S(2)}) collective-permute-start(bf16[320,4,1,128]{3,0,2,1:T(8,128)(2,1)S(1)} %slice.707), channel_id=1, source_target_pairs={{0,31},{1,0},{2,1},{3,2},{4,3},{5,4},{6,5},{7,6},{8,7},{9,8},{10,9... | collective-permute-start | bytes 983048 | tf_op jit(solution)/shard_map/ppermute | solution.py:28
Sparse Core Ops, SparseCore 0:
  34.0 35.2 all-gather.4
  110.5 36.4 all-gather.4
  188.2 36.4 all-gather.4
  265.9 36.4 all-gather.4
  343.6 36.4 all-gather.4
  421.3 36.4 all-gather.4
  499.0 36.4 all-gather.4
  576.7 36.4 all-gather.4
